TPU v7x, 256 devices: a whole 4x4x8 slice. The times are simulated.
256 devices in a mesh: wide: 16 (over x, y), narrow: 16 (over z, core).
Axes of the slice: x: 4, y: 4, z: 8, core: 2. Of those that a mesh axis runs over, the one named last changes fastest.
Arguments:
- field: float32 [11, 384, 512, 128], P(None, 'wide', 'narrow'), may hold values from -110 to 110, as said below
- start_x: float32 [384, 64], replicated, may hold values from -0.3125 to 0.3125
- start_y: float32 [512, 64], replicated, may hold values from -0.25 to 0.25
- start_z: float32 [128, 64], replicated, may hold values from -0.5 to 0.5
Outputs:
- core_block: float32 [11, 64, 64, 64], P(None, 'narrow', 'wide')
- factor_x: float32 [384, 64], replicated
- factor_y: float32 [512, 64], replicated
- factor_z: float32 [128, 64], replicated
Inputs may be any that keep to these rules, and one draw needn't show every extreme that they name: Real-valued field.
All inputs are finite; a program needn't handle non-finite values.
Results may differ from a plain program's by a relative error of at most 0.00024.
Values sent between devices are 32-bit elements; how exact they have to be, the bound alone decides.
A program may use at most 128 MiB of HBM per device.

v0:
```python
import jax
import jax.numpy as jnp
from jax import lax
from jax.sharding import Mesh
from jax.sharding import PartitionSpec as P

ITERS = 2
WIDE = ("wide_0", "wide_1")
NARROW = ("narrow_0", "narrow_1")


def in_blocks(shard, dim, devices):
    before, after = (shard.shape[:dim], shard.shape[dim + 1 :])
    return jnp.moveaxis(shard.reshape(*before, devices, -1, *after), dim, 0)


def summed_on_arrival(shard, axis, dim):
    pieces = in_blocks(shard, dim, lax.axis_size(axis))
    arrived = lax.all_to_all(pieces, axis, split_axis=0, concat_axis=0, tiled=True)
    return arrived.sum(axis=0)


def sum_by_axis(shard, axes, dim):
    far, near = axes
    pieces = in_blocks(shard, dim, lax.axis_size(far))
    nearer = summed_on_arrival(pieces, near, dim + 1)
    arrived = lax.all_to_all(nearer, far, split_axis=0, concat_axis=0, tiled=True)
    return arrived.sum(axis=0)


def rows_for(lines, devices):
    spare = -len(lines) % devices
    return jnp.pad(lines, [(0, spare)] + [(0, 0)] * (lines.ndim - 1))


def from_everyone(shard, axis):
    devices = lax.axis_size(axis)
    return lax.all_to_all(
        jnp.broadcast_to(shard[None], (devices, *shard.shape)), axis, 0, 0, tiled=True
    )


def in_order(pieces, dim):
    shape = list(pieces.shape[1:])
    shape[dim] *= pieces.shape[0]
    return jnp.moveaxis(pieces, 0, dim).reshape(shape)


def gather_axes(shard, axes, dim):
    far, near = axes
    pieces = from_everyone(from_everyone(shard, far), near)
    return in_order(pieces.swapaxes(0, 1).reshape(-1, *shard.shape), dim)


def nested_sum(shard, axes):
    lines = shard.reshape(-1)
    own = sum_by_axis(rows_for(lines, lax.axis_size(axes[0]) * lax.axis_size(axes[1])), axes, 0)
    whole = gather_axes(own, axes, 0)
    return whole[: len(lines)].reshape(shard.shape)


def gram_of(block_data, contracted):
    part_gram = lax.dot_general(
        block_data,
        block_data,
        ((contracted, contracted), ((), ())),
        precision=lax.Precision.HIGHEST,
    )
    return nested_sum(part_gram, ("wide_0", ("wide_1", "narrow_0", "narrow_1")))


def subspace(gram_full, start_cols):
    basis_now = start_cols
    for step_index in range(ITERS):
        image_cols = jnp.dot(gram_full, basis_now, precision=lax.Precision.HIGHEST)
        inner_prod = jnp.dot(image_cols.T, image_cols, precision=lax.Precision.HIGHEST)
        lower_tri = jnp.linalg.cholesky(inner_prod)
        basis_now = jax.scipy.linalg.solve_triangular(lower_tri, image_cols.T, lower=True).T
    return basis_now


def body(field, start_x, start_y, start_z):
    whole_x = lax.all_to_all(field, WIDE, split_axis=3, concat_axis=1, tiled=True)
    factor_x = subspace(gram_of(whole_x, (0, 2, 3)), start_x)
    shrunk = jnp.einsum("sxyz,xr->sryz", whole_x, factor_x, precision=lax.Precision.HIGHEST)
    whole_y = lax.all_to_all(shrunk, NARROW, split_axis=1, concat_axis=2, tiled=True)
    factor_y = subspace(gram_of(whole_y, (0, 1, 3)), start_y)
    second = jnp.einsum("sxyz,yr->sxrz", whole_y, factor_y, precision=lax.Precision.HIGHEST)
    whole_z = lax.all_to_all(second, WIDE, split_axis=2, concat_axis=3, tiled=True)
    factor_z = subspace(gram_of(whole_z, (0, 1, 2)), start_z)
    core_block = jnp.einsum("sxyz,zr->sxyr", whole_z, factor_z, precision=lax.Precision.HIGHEST)
    return (core_block, factor_x, factor_y, factor_z)


def solution(mesh):
    split = Mesh(mesh.devices.reshape(4, 4, 8, 2), ("wide_0", "wide_1", "narrow_0", "narrow_1"))
    placed = (P(None, WIDE, NARROW, None), P(), P(), P())
    return jax.shard_map(
        body,
        mesh=split,
        in_specs=placed,
        out_specs=(P(None, NARROW, WIDE, None), P(), P(), P()),
        check_vma=False,
    )
```

profile of v0, /device:TPU:1, one launch (start us, length us, event | category | flops | bytes accessed | tf_op | source)
XLA Modules:
  0.0 532.9 jit_solution(8270564081755581063)
XLA Ops:
  0.6 16.0 %copy.40 = f32[11,24,32,128]{2,1,0,3:T(8,128)} copy(f32[11,24,32,128]{3,2,1,0:T(8,128)} %param.11) | data formatting | bytes 8650752 | tf_op args[0]
  16.6 16.3 %reshape.65 = f32[16,1,67584]{2,1,0:T(1,128)} reshape(f32[128,11,24,32]{3,2,1,0:T(8,128)} %bitcast.185) | data formatting | bytes 8650752
  32.9 59.3 %all_to_all.129 = f32[16,1,67584]{2,1,0:T(1,128)} all-to-all(f32[16,1,67584]{2,1,0:T(1,128)} %reshape.65), channel_id=1, replica_groups=mesh['wide_0'=4,'wide_1'=4,'narrow_0'=8,'narrow_1'=2] {'wide_0','wide_1'}, dimensions={0} | all-to-all | bytes 8650752 | tf_op jit(solution)/shard_map/all_to_all | solution.py:83
  92.7 14.1 %reduce.7 = f32[16,67584]{1,0:T(8,128)} reduce(f32[16,1,67584]{2,1,0:T(1,128)} %all_to_all.129, f32[]{:T(128)} %broadcast.69), dimensions={1}, to_apply=%all_to_all.87.reduce_sub_computation | reduce | bytes 8650756 | tf_op jit(solution)/shard_map/all_to_all | solution.py:83
  106.8 15.6 %reshape.66 = f32[128,11,24,32]{3,2,1,0:T(8,128)} reshape(f32[16,67584]{1,0:T(8,128)} %reduce.7) | data formatting | bytes 8650752
  122.4 21.3 %copy.42 = f32[11,16,24,32,8]{2,1,4,3,0:T(8,128)} copy(f32[11,16,24,32,8]{3,2,0,4,1:T(8,128)} %bitcast.184) | data formatting | bytes 8650752 | tf_op jit(solution)/shard_map/all_to_all | solution.py:83
  143.8 18.3 %all_to_all.90 = f32[11,384,32,8]{1,3,2,0:T(8,128)} reshape(f32[11,16,24,32,8]{2,1,4,3,0:T(8,128)} %copy.42) | data formatting | bytes 8650752 | tf_op jit(solution)/shard_map/all_to_all | solution.py:83
  162.1 10.5 %convolution_bitcast_fusion.1 = f32[384,384]{1,0:T(8,128)S(1)} fusion(f32[11,384,32,8]{1,3,2,0:T(8,128)} %all_to_all.90), kind=kOutput, calls=%fused_computation.4 | convolution fusion | flops 4982833152 | bytes 4915200 | tf_op jit(solution)/shard_map/dot_general | solution.py:63
  173.4 31.9 %all_to_all.130 = f32[64,4,576]{2,1,0:T(4,128)S(1)} all-to-all(f32[64,4,576]{2,1,0:T(4,128)S(1)} %bitcast.192), channel_id=1, replica_groups=mesh['wide_0'=4,'wide_1'=4,'narrow_0'=8,'narrow_1'=2] {'wide_1','narrow_..., dimensions={0} | all-to-all | bytes 1179648 | tf_op jit(solution)/shard_map/all_to_all | solution.py:19
  205.5 6.5 %all_to_all.131 = f32[4,1,576]{2,1,0:T(1,128)S(1)} all-to-all(f32[4,1,576]{2,1,0:T(1,128)S(1)} %all_to_all.92), channel_id=1, replica_groups=mesh['wide_0'=4,'wide_1'=4,'narrow_0'=8,'narrow_1'=2] {'wide_0'}, dimensions={0} | all-to-all | bytes 18432 | tf_op jit(solution)/shard_map/all_to_all | solution.py:27
  212.0 6.5 %all_to_all.132 = f32[4,1,576]{2,1,0:T(1,128)S(1)} all-to-all(f32[4,1,576]{2,1,0:T(1,128)S(1)} %broadcast_in_dim.19), channel_id=1, replica_groups=mesh['wide_0'=4,'wide_1'=4,'narrow_0'=8,'narrow_1'=2] {'wide_0'}, dimensions={0} | all-to-all | bytes 18432 | tf_op jit(solution)/shard_map/all_to_all | solution.py:38
  218.6 29.0 %all_to_all.133 = f32[64,4,576]{2,1,0:T(4,128)S(1)} all-to-all(f32[64,4,576]{2,1,0:T(4,128)S(1)} %broadcast_in_dim.21), channel_id=1, replica_groups=mesh['wide_0'=4,'wide_1'=4,'narrow_0'=8,'narrow_1'=2] {'wide_1','narrow_..., dimensions={0} | all-to-all | bytes 1179648 | tf_op jit(solution)/shard_map/all_to_all | solution.py:38
  249.2 5.8 %cholesky.104 = f32[64,64]{1,0:T(8,128)S(1)} custom-call(f32[64,64]{1,0:T(8,128)S(1)} %fusion.39), custom_call_target="Cholesky" | custom-call | tf_op jit(solution)/shard_map/jit(cholesky)/cholesky | solution.py:77
  275.1 7.6 %fusion.2 = f32[11,64,32,8]{1,2,3,0:T(8,128)} fusion(f32[11,384,32,8]{1,3,2,0:T(8,128)} %all_to_all.90, f32[64,384]{1,0:T(8,128)S(1)} %fusion.12), kind=kOutput, calls=%fused_computation.2 | convolution fusion | flops 830472192 | bytes 5144576 | tf_op jit(solution)/shard_map/sxyz,xr->sryz/dot_general | solution.py:85
  287.6 26.1 %all_to_all.134 = f32[16,1,11264]{2,1,0:T(1,128)S(1)} all-to-all(f32[16,1,11264]{2,1,0:T(1,128)} %reshape.67), channel_id=1, replica_groups=mesh['wide_0'=4,'wide_1'=4,'narrow_0'=8,'narrow_1'=2] {'narrow_0','narro..., dimensions={0} | all-to-all | bytes 1441792 | tf_op jit(solution)/shard_map/all_to_all | solution.py:86
  327.8 32.7 %all_to_all.135 = f32[64,4,1024]{2,1,0:T(4,128)S(1)} all-to-all(f32[64,4,1024]{2,1,0:T(4,128)S(1)} %bitcast.189), channel_id=1, replica_groups=mesh['wide_0'=4,'wide_1'=4,'narrow_0'=8,'narrow_1'=2] {'wide_1','narrow_..., dimensions={0} | all-to-all | bytes 2097152 | tf_op jit(solution)/shard_map/all_to_all | solution.py:19
  360.8 6.6 %all_to_all.136 = f32[4,1,1024]{2,1,0:T(1,128)S(1)} all-to-all(f32[4,1,1024]{2,1,0:T(1,128)S(1)} %all_to_all.101), channel_id=1, replica_groups=mesh['wide_0'=4,'wide_1'=4,'narrow_0'=8,'narrow_1'=2] {'wide_0'}, dimensions={0} | all-to-all | bytes 32768 | tf_op jit(solution)/shard_map/all_to_all | solution.py:27
  367.4 6.6 %all_to_all.137 = f32[4,1,1024]{2,1,0:T(1,128)S(1)} all-to-all(f32[4,1,1024]{2,1,0:T(1,128)S(1)} %broadcast_in_dim.22), channel_id=1, replica_groups=mesh['wide_0'=4,'wide_1'=4,'narrow_0'=8,'narrow_1'=2] {'wide_0'}, dimensions={0} | all-to-all | bytes 32768 | tf_op jit(solution)/shard_map/all_to_all | solution.py:38
  374.2 37.0 %all_to_all.138 = f32[64,4,1024]{2,1,0:T(4,128)S(1)} all-to-all(f32[64,4,1024]{2,1,0:T(4,128)S(1)} %broadcast_in_dim.24), channel_id=1, replica_groups=mesh['wide_0'=4,'wide_1'=4,'narrow_0'=8,'narrow_1'=2] {'wide_1','narrow_..., dimensions={0} | all-to-all | bytes 2097152 | tf_op jit(solution)/shard_map/all_to_all | solution.py:38
  442.8 11.4 %all_to_all.139 = f32[16,1,1408]{2,1,0:T(1,128)S(1)} all-to-all(f32[16,1,1408]{2,1,0:T(1,128)S(1)} %reshape.69), channel_id=1, replica_groups=mesh['wide_0'=4,'wide_1'=4,'narrow_0'=8,'narrow_1'=2] {'wide_0','wide_1'}, dimensions={0} | all-to-all | bytes 180224 | tf_op jit(solution)/shard_map/all_to_all | solution.py:89
  459.2 15.5 %all_to_all.140 = f32[64,1,256]{2,1,0:T(1,128)S(1)} all-to-all(f32[64,1,256]{2,1,0:T(1,128)S(1)} %reshape.71), channel_id=1, replica_groups=mesh['wide_0'=4,'wide_1'=4,'narrow_0'=8,'narrow_1'=2] {'wide_1','narrow_..., dimensions={0} | all-to-all | bytes 131072 | tf_op jit(solution)/shard_map/all_to_all | solution.py:19
  475.7 6.5 %all_to_all.141 = f32[4,1,64]{2,1,0:T(1,128)S(1)} all-to-all(f32[4,1,64]{2,1,0:T(1,128)S(1)} %bitcast.201), channel_id=1, replica_groups=mesh['wide_0'=4,'wide_1'=4,'narrow_0'=8,'narrow_1'=2] {'wide_0'}, dimensions={0} | all-to-all | bytes 2048 | tf_op jit(solution)/shard_map/all_to_all | solution.py:27
  482.2 6.5 %all_to_all.142 = f32[4,1,64]{2,1,0:T(1,128)S(1)} all-to-all(f32[4,1,64]{2,1,0:T(1,128)S(1)} %broadcast_in_dim.25), channel_id=1, replica_groups=mesh['wide_0'=4,'wide_1'=4,'narrow_0'=8,'narrow_1'=2] {'wide_0'}, dimensions={0} | all-to-all | bytes 2048 | tf_op jit(solution)/shard_map/all_to_all | solution.py:38
  488.8 15.9 %all_to_all.143 = f32[64,1,256]{2,1,0:T(1,128)S(1)} all-to-all(f32[64,1,256]{2,1,0:T(1,128)S(1)} %reshape.73), channel_id=1, replica_groups=mesh['wide_0'=4,'wide_1'=4,'narrow_0'=8,'narrow_1'=2] {'wide_1','narrow_..., dimensions={0} | all-to-all | bytes 131072 | tf_op jit(solution)/shard_map/all_to_all | solution.py:38
  (123 shorter events, 107.6 us)
Async XLA Ops:
  0.6 411.4 %copy-start = (f32[512,64]{0,1:T(8,128)S(1)}, f32[512,64]{0,1:T(8,128)}, u32[]{:S(2)}) copy-start(f32[512,64]{0,1:T(8,128)} %param.13) | copy-start | bytes 393220
  172.6 75.5 %copy-start.4 = (f32[384,64]{0,1:T(8,128)S(1)}, f32[384,64]{0,1:T(8,128)}, u32[]{:S(2)}) copy-start(f32[384,64]{0,1:T(8,128)} %param.12) | copy-start | bytes 294916
  275.1 10.3 %copy-start.2 = (f32[64,384]{1,0:T(8,128)}, f32[64,384]{1,0:T(8,128)S(1)}, u32[]{:S(2)}) copy-start(f32[64,384]{1,0:T(8,128)S(1)} %fusion.12) | copy-start | bytes 294916
  439.9 18.6 %copy-start.1 = (f32[64,512]{1,0:T(8,128)}, f32[64,512]{1,0:T(8,128)S(1)}, u32[]{:S(2)}) copy-start(f32[64,512]{1,0:T(8,128)S(1)} %fusion.7) | copy-start | bytes 393220
  442.8 63.0 %copy-start.5 = (f32[128,64]{0,1:T(8,128)S(1)}, f32[128,64]{0,1:T(8,128)}, u32[]{:S(2)}) copy-start(f32[128,64]{0,1:T(8,128)} %param.14) | copy-start | bytes 98308
  531.5 1.0 copy-start.3
where the time goes:
time: 541 us; the launch traced here: 533 us
  blocking collectives  298 us (55%)
  local copies, waits for them, and re-layouts  111 us (21%)
  other arithmetic  92.9 us (17%)
  matrix products  29.2 us (5%)
    all_to_all x6, blocking collectives, from_everyone(): lax.all_to_all(jnp.broadcast_to(shard[None], (devices, *shard.shape)), ax...  102 us
    all_to_all x3, blocking collectives, summed_on_arrival(): lax.all_to_all(pieces, axis, split_axis=0, concat_axis=0, tiled=True)  80.1 us
    all_to_all x1, blocking collectives, body(): lax.all_to_all(field, WIDE, split_axis=3, concat_axis=1, tiled=True)  59.3 us
    unnamed x26, local copies, waits for them, and re-layouts  54.9 us
    all_to_all x3, local copies, waits for them, and re-layouts, body(): lax.all_to_all(field, WIDE, split_axis=3, concat_axis=1, tiled=True)  40.2 us
    another operation x18, other arithmetic, subspace(): lower_tri = jnp.linalg.cholesky(inner_prod)  39.1 us
    another operation x12, other arithmetic, subspace(): jax.scipy.linalg.solve_triangular(lower_tri, image_cols.T, lower=True)  33.3 us
    all_to_all x1, blocking collectives, body(): lax.all_to_all(shrunk, NARROW, split_axis=1, concat_axis=2, tiled=True)  26.1 us

commit v1 on v0

v1 whole, which is shorter than its diff:
```python
import functools

import jax
import jax.numpy as jnp
from jax import lax
from jax.experimental import pallas as pl
from jax.experimental.pallas import tpu as pltpu
from jax.sharding import PartitionSpec as P

ITERS = 2
MESH = pl.DeviceIdType.MESH
HIGH = lax.Precision.HIGHEST
F32 = jnp.float32
BF16 = jnp.bfloat16

S, X, Y, Z, R = 11, 384, 512, 128, 64
WX, WY = 4, 4
NW, NN = 16, 16
XB = X // NW
J = 3
NT = (((1,), (1,)), ((), ()))
TN = (((0,), (0,)), ((), ()))


def dot(a, b, dims=(((1,), (0,)), ((), ())), precision=None):
    return lax.dot_general(a, b, dims, precision=precision, preferred_element_type=F32)


def split(v):
    high = v.astype(BF16)
    return high, (v - high.astype(F32)).astype(BF16)


def pairs(size):
    blocks = size // 128
    return [(i, j) for i in range(blocks) for j in range(i, blocks)]


def block(i):
    return slice(i * 128, (i + 1) * 128)


def kernel(
    field, start_x, start_y, start_z,
    core_out, out_x, out_y, out_z,
    fibres, fib_hi, fib_lo, acc_hh, acc_hl,
    shrunk, columns, col_hi, col_lo, second, regrouped,
    part_x, arrive_x, own_x, near_x, mid_x, full_x,
    part_y, arrive_y, own_y, near_y, mid_y, full_y,
    part_z, arrive_z, own_z, near_z, mid_z, full_z,
    gram, basis, elim,
    send_a, recv_a, local_a,
    send_c, recv_c, local_c,
    send_d, recv_d, local_d,
    send_g, recv_g,
):
    w = lax.axis_index("wide")
    n = lax.axis_index("narrow")
    wx, wy = w // WY, w % WY

    barrier = pltpu.get_barrier_semaphore()

    def greet(wide, narrow):
        pl.semaphore_signal(barrier, inc=1, device_id=(wide, narrow), device_id_type=MESH)

    @pl.loop(1, NW)
    def _(d):
        greet((w + d) % NW, n)
        greet(w, (n + d) % NN)

    @pl.loop(1, WY)
    def _(dy):
        @pl.loop(1, NN)
        def _(dn):
            greet(wx * WY + (wy + dy) % WY, (n + dn) % NN)

    pl.semaphore_wait(barrier, 2 * (NW - 1) + (WY - 1) * (NN - 1))

    def remote(src, dst, send, recv, wide, narrow):
        return pltpu.make_async_remote_copy(
            src_ref=src, dst_ref=dst, send_sem=send, recv_sem=recv,
            device_id=(wide, narrow), device_id_type=MESH,
        )

    def await_recv(ref, sem):
        remote(ref, ref, sem, sem, w, n).wait_recv()

    def await_send(ref, sem):
        remote(ref, ref, sem, sem, w, n).wait_send()

    mine = pl.ds(w * XB, XB)

    for j in range(J):
        @pl.loop(1, NW)
        def _(d, j=j):
            t = (w + d) % NW
            species = t // WY + WX * j

            @pl.when(species < S)
            def _():
                remote(
                    field.at[species, :, t % WY], fibres.at[j, mine],
                    send_a, recv_a.at[j], t, n,
                ).start()

        @pl.when(wx + WX * j < S)
        def _(j=j):
            pltpu.make_async_copy(
                field.at[wx + WX * j, :, wy], fibres.at[j, mine], local_a.at[j]
            ).start()

    for j in range(J):
        @pl.when(wx + WX * j < S)
        def _(j=j):
            pltpu.make_async_copy(
                field.at[wx + WX * j, :, wy], fibres.at[j, mine], local_a.at[j]
            ).wait()
            await_recv(fibres.at[j, pl.ds(0, (NW - 1) * XB)], recv_a.at[j])

        @pl.when(wx + WX * j >= S)
        def _(j=j):
            fibres[j] = jnp.zeros(fibres.shape[1:], F32)

        lines = fibres.at[j].reshape(X * 8, Z)
        for y in range(8):
            high, low = split(lines[pl.ds(y, X, stride=8), :])
            fib_hi[j, :, block(y)] = high
            fib_lo[j, :, block(y)] = low
        high = fib_hi[j]
        hh = dot(high, high, NT)
        hl = dot(high, fib_lo[j], NT)
        acc_hh[:X, :X] = hh if j == 0 else acc_hh[:X, :X] + hh
        acc_hl[:X, :X] = hl if j == 0 else acc_hl[:X, :X] + hl

    def pack(size, part):
        for b, (i, j) in enumerate(pairs(size)):
            part[block(b), :] = (
                acc_hh[block(i), block(j)] + acc_hl[block(i), block(j)]
                + acc_hl[block(j), block(i)].T
            )

    def unpack(size, full):
        for b, (i, j) in enumerate(pairs(size)):
            one = full[block(b), :]
            gram[block(i), block(j)] = one
            if i != j:
                gram[block(j), block(i)] = one.T

    def all_reduce(mode, tiles, part, arrive, own, near, mid, full):
        rows = tiles * 8

        def share(which):
            return pl.ds(pl.multiple_of(which * rows, 8), rows)

        send = send_g.at[mode]

        @pl.loop(1, NW)
        def _(d):
            t = (w + d) % NW
            remote(part.at[share(t)], arrive.at[share(w)], send.at[0], recv_g.at[mode, 0], t, n).start()

        arrive[share(w), :] = part[share(w), :]
        await_recv(arrive.at[pl.ds(0, (NW - 1) * rows)], recv_g.at[mode, 0])
        total = arrive[pl.ds(0, rows), :]
        for t in range(1, NW):
            total = total + arrive[pl.ds(t * rows, rows), :]
        if tiles == 1:
            own[...] = total

            @pl.loop(1, NN)
            def _(d):
                t = (n + d) % NN
                remote(own, near.at[n], send.at[1], recv_g.at[mode, 1], w, t).start()

            near[n] = total
            await_recv(near.at[pl.ds(0, NN - 1)], recv_g.at[mode, 1])
            total = near[0]
            for t in range(1, NN):
                total = total + near[t]
            mid[0] = total
            await_send(near.at[pl.ds(0, NN - 1)], send.at[1])
        else:
            for t in range(tiles):
                own[t] = total[t * 8 : (t + 1) * 8]

            @pl.loop(0, tiles)
            def _(t):
                @pl.when(t != n)
                def _():
                    remote(own.at[t], near.at[n], send.at[1], recv_g.at[mode, 1], w, t).start()

            @pl.when(n < tiles)
            def _():
                near[n] = own[n]
                await_recv(near.at[pl.ds(0, NN - 1)], recv_g.at[mode, 1])
                final = near[0]
                for t in range(1, NN):
                    final = final + near[t]
                mid[n] = final

                @pl.loop(1, NN)
                def _(d):
                    t = (n + d) % NN
                    remote(mid.at[n], mid.at[n], send.at[2], recv_g.at[mode, 2], w, t).start()

                await_recv(mid.at[pl.ds(0, tiles - 1)], recv_g.at[mode, 2])
                await_send(near.at[pl.ds(0, NN - 1)], send.at[2])
                await_send(near.at[pl.ds(0, tiles - 1)], send.at[1])

            @pl.when(n >= tiles)
            def _():
                await_recv(mid.at[pl.ds(0, tiles)], recv_g.at[mode, 2])
                await_send(near.at[pl.ds(0, tiles)], send.at[1])

        @pl.loop(1, NW)
        def _(d):
            t = (w + d) % NW
            remote(mid, full.at[w], send.at[3], recv_g.at[mode, 3], t, n).start()

        full[w] = mid[...]
        await_recv(full.at[pl.ds(0, NW - 1)], recv_g.at[mode, 3])
        await_send(full.at[pl.ds(0, NW - 1)], send.at[3])
        await_send(arrive.at[pl.ds(0, (NW - 1) * rows)], send.at[0])

    row_of = lax.broadcasted_iota(jnp.int32, (R, 128), 0)
    line_of = lax.broadcasted_iota(jnp.int32, (8, 128), 0)

    def lower_inverse(inner):
        here = lax.broadcasted_iota(jnp.int32, (R, R), 0)
        there = lax.broadcasted_iota(jnp.int32, (R, R), 1)
        elim[:, :R] = inner
        elim[:, R:] = (here == there).astype(F32)

        def step(b, _):
            start = pl.multiple_of(b * 8, 8)
            whole = elim[...]
            panel = elim[pl.ds(start, 8), :]
            below = row_of >= (b + 1) * 8
            for i in range(8):
                row = panel[i : i + 1, :]
                scale = lax.rsqrt(row[:, i : i + 1])
                row = row * scale
                panel = jnp.where(
                    line_of == i, jnp.broadcast_to(row, (8, 128)),
                    panel - jnp.where(line_of > i, panel[:, i : i + 1] * scale, 0.0) * row,
                )
                whole = whole - jnp.where(below, whole[:, i : i + 1] * scale, 0.0) * row
            elim[...] = pltpu.roll(whole, 120, 1)
            elim[pl.ds(start, 8), :] = pltpu.roll(panel, 120, 1)
            return 0

        lax.fori_loop(0, R // 8, step, 0)
        return elim[:, :R]

    def subspace(size, start, out):
        basis[:size, :] = start[...]

        def turn(_, carry):
            image = dot(gram[:size, :size], basis[:size, :], precision=HIGH)
            inner = dot(image, image, TN, HIGH)
            basis[:size, :] = dot(image, lower_inverse(inner), NT, HIGH)
            return carry

        lax.fori_loop(0, ITERS, turn, 0)
        out[...] = basis[:size, :]

    pack(X, part_x)
    all_reduce(0, 6, part_x, arrive_x, own_x, near_x, mid_x, full_x)
    unpack(X, full_x.reshape(6 * 128, 128))
    subspace(X, start_x, out_x)

    high, low = split(basis[:X, :].T)
    slab = wx * WY
    for j in range(J):
        part = dot(high, fib_hi[j]) + dot(high, fib_lo[j]) + dot(low, fib_hi[j])
        lines = shrunk.at[j].reshape(R * 8, Z)
        for y in range(8):
            lines[pl.ds(y, R, stride=8), :] = part[:, block(y)]

        @pl.when(wx + WX * j < S)
        def _(j=j):
            @pl.loop(1, R)
            def _(d):
                t = (n * WY + wy + d) % R
                remote(
                    shrunk.at[j, t], columns.at[j, n * WY + wy], send_c, recv_c.at[j],
                    slab + t % WY, t // WY,
                ).start()

            columns[j, n * WY + wy] = shrunk[j, n * WY + wy]

    for j in range(J):
        @pl.when(wx + WX * j < S)
        def _(j=j):
            await_recv(columns.at[j, pl.ds(0, R - 1)], recv_c.at[j])

        @pl.when(wx + WX * j >= S)
        def _(j=j):
            columns[j] = jnp.zeros(columns.shape[1:], F32)

        high, low = split(columns[j].reshape(Y, Z))
        col_hi[:, block(j)] = high
        col_lo[:, block(j)] = low
    high = col_hi[...]
    acc_hh[...] = dot(high, high, NT)
    acc_hl[...] = dot(high, col_lo[...], NT)
    pack(Y, part_y)
    all_reduce(1, 10, part_y, arrive_y, own_y, near_y, mid_y, full_y)
    unpack(Y, full_y.reshape(10 * 128, 128))
    subspace(Y, start_y, out_y)

    row = lax.broadcasted_iota(jnp.int32, (2 * R, R), 0)
    col = lax.broadcasted_iota(jnp.int32, (2 * R, R), 1)
    spread = ((row % 8 < 4) & (row // 8 * 4 + row % 8 == col)).astype(F32)
    high, low = split(dot(spread, basis[:Y, :], NT, HIGH))
    part = dot(high, col_hi[...]) + dot(high, col_lo[...]) + dot(low, col_hi[...])
    total = jnp.zeros((Z, Z), F32)
    for j in range(J):
        one = part[:, block(j)]
        second[j] = one.reshape(NW, 8, Z)
        total = total + dot(one, one, TN, HIGH)
    part_z[...] = total

    @pl.loop(1, NW)
    def _(d):
        t = (w + d) % NW
        remote(second.at[:, t], regrouped.at[:, w], send_d, recv_d, t, n).start()

    for j in range(J):
        regrouped[j, w] = second[j, w]
    all_reduce(2, 1, part_z, arrive_z, own_z, near_z, mid_z, full_z)
    gram[:Z, :Z] = full_z[...].reshape(Z, Z)
    subspace(Z, start_z, out_z)

    await_recv(regrouped.at[:, pl.ds(0, NW - 1)], recv_d)
    core_out[...] = dot(regrouped[...].reshape(J * NW * 8, Z), basis[:Z, :], precision=HIGH)

    await_send(regrouped.at[:, pl.ds(0, NW - 1)], send_d)
    for j in range(J):
        @pl.when(wx + WX * j < S)
        def _(j=j):
            await_send(columns.at[j, pl.ds(0, R - 1)], send_c)
    for j in range(J - 1):
        await_send(fibres.at[j, pl.ds(0, (NW - 1) * XB)], send_a)
    last = WY * (S - WX * (J - 1))

    @pl.when(wx + WX * (J - 1) < S)
    def _():
        await_send(fibres.at[J - 1, pl.ds(0, (last - 1) * XB)], send_a)

    @pl.when(wx + WX * (J - 1) >= S)
    def _():
        await_send(fibres.at[J - 1, pl.ds(0, last * XB)], send_a)


def reduce_scratch(tiles):
    rows = tiles * 128
    return [
        pltpu.VMEM((rows, 128), F32),
        pltpu.VMEM((rows, 128), F32),
        pltpu.VMEM((tiles, 8, 128) if tiles > 1 else (8, 128), F32),
        pltpu.VMEM((NN, 8, 128), F32),
        pltpu.VMEM((tiles, 8, 128), F32),
        pltpu.VMEM((NW, tiles, 8, 128), F32),
    ]


def body(field, start_x, start_y, start_z):
    vmem = pl.BlockSpec(memory_space=pltpu.VMEM)
    dma = pltpu.SemaphoreType.DMA
    core, fx, fy, fz = pl.pallas_call(
        kernel,
        out_shape=(
            jax.ShapeDtypeStruct((J * NW * 8, R), F32),
            jax.ShapeDtypeStruct((X, R), F32),
            jax.ShapeDtypeStruct((Y, R), F32),
            jax.ShapeDtypeStruct((Z, R), F32),
        ),
        in_specs=[pl.BlockSpec(memory_space=pl.ANY), vmem, vmem, vmem],
        out_specs=(vmem,) * 4,
        scratch_shapes=[
            pltpu.VMEM((J, X, 8, Z), F32),
            pltpu.VMEM((J, X, 8 * Z), BF16),
            pltpu.VMEM((J, X, 8 * Z), BF16),
            pltpu.VMEM((Y, Y), F32),
            pltpu.VMEM((Y, Y), F32),
            pltpu.VMEM((J, R, 8, Z), F32),
            pltpu.VMEM((J, R, 8, Z), F32),
            pltpu.VMEM((Y, J * Z), BF16),
            pltpu.VMEM((Y, J * Z), BF16),
            pltpu.VMEM((J, NW, 8, Z), F32),
            pltpu.VMEM((J, NW, 8, Z), F32),
            *reduce_scratch(6),
            *reduce_scratch(10),
            *reduce_scratch(1),
            pltpu.VMEM((Y, Y), F32),
            pltpu.VMEM((Y, R), F32),
            pltpu.VMEM((R, 128), F32),
            dma, dma((J,)), dma((J,)),
            dma, dma((J,)), dma,
            dma, dma, dma,
            dma((3, 4)), dma((3, 4)),
        ],
        compiler_params=pltpu.CompilerParams(collective_id=0, has_side_effects=True),
    )(field.reshape(S, XB, WY, 8, Z), start_x, start_y, start_z)
    core = core.reshape(WX * J, NN // 4, 8, R)[:S, :, :4, :]
    return core, fx, fy, fz


def solution(mesh):
    return jax.shard_map(
        body,
        mesh=mesh,
        in_specs=(P(None, "wide", "narrow", None), P(), P(), P()),
        out_specs=(P(None, "narrow", "wide", None), P(), P(), P()),
        check_vma=False,
    )
```

time: 541 us -> 231 us (0.43); the launches traced: 533 us -> 231 us
  blocking collectives: 298 us -> 0 us
  Pallas kernels: 0 us -> 219 us
  local copies, waits for them, and re-layouts: 111 us -> 11.4 us
  other arithmetic: 92.9 us -> 0 us
  matrix products: 29.2 us -> 0 us
    all_to_all x15 -> x0, blocking collectives: 298 us -> none  [the longest x6 102 us: from_everyone(): lax.all_to_all(jnp.broadcast_to(shard[None], (devices, *shard.shape)), ax...]
    pallas_call x0 -> x1, Pallas kernels: none -> 219 us  [body(): pl.pallas_call(kernel, out_shape=(jax.ShapeDtypeStruct((J * NW * 8, R), F...]
    another operation x30 -> x0, other arithmetic: 72.4 us -> none  [the longest x18 39.1 us: subspace(): lower_tri = jnp.linalg.cholesky(inner_prod)]
    all_to_all x9 -> x0, local copies, waits for them, and re-layouts: 48.4 us -> none  [the longest x3 40.2 us: body(): lax.all_to_all(field, WIDE, split_axis=3, concat_axis=1, tiled=True)]
    unnamed x26 -> x6, local copies, waits for them, and re-layouts: 54.9 us -> 9.86 us
    dot_general x18 -> x0, matrix products: 27.4 us -> none  [the longest x3 12.8 us: gram_of(): lax.dot_general(block_data, block_data, ((contracted, contracted), ((), (...]
    all_to_all x5 -> x0, other arithmetic: 20 us -> none  [the longest x1 14.1 us: body(): lax.all_to_all(field, WIDE, split_axis=3, concat_axis=1, tiled=True)]
where the time goes in v1:
time: 231 us
  Pallas kernels  219 us (95%)
  local copies, waits for them, and re-layouts  11.4 us (5%)
    pallas_call x1, Pallas kernels, body(): pl.pallas_call(kernel, out_shape=(jax.ShapeDtypeStruct((J * NW * 8, R), F...  219 us
    unnamed x6, local copies, waits for them, and re-layouts  9.86 us

profile of v1, /device:TPU:1, one launch (start us, length us, event | category | flops | bytes accessed | tf_op | source)
XLA Modules:
  0.0 231.0 jit_solution(7781128846945133386)
XLA Ops:
  0.6 1.5 copy.10.start_z
  2.1 1.7 copy.8.start_x
  3.8 1.7 copy.9.start_y
  5.5 219.0 %shard_map.75 = (f32[384,64]{1,0:T(8,128)}, f32[384,64]{1,0:T(8,128)}, f32[512,64]{1,0:T(8,128)}, f32[128,64]{1,0:T(8,128)}) custom-call(f32[11,24,4,8,128]{4,3,2,1,0:T(8,128)} %bitcast.2, f32[384,64]{1,0:T(8,128)} %copy.8.start_x, f32[512,64]{1,0:T(8,128)} %copy.9.start_y, f32[128,64]{1,0:T(8,128)} %copy.10.start_z), custom_call_target="tpu_custom_call" | custom-call | tf_op jit(solution)/shard_map/pallas_call | solution.py:371
  224.5 1.6 slice.4
  226.1 1.5 copy.13
  227.6 1.7 copy.11
  229.3 1.7 copy.12

commit v2 on v1

v2 whole, which is shorter than its diff:
```python
import functools

import jax
import jax.numpy as jnp
from jax import lax
from jax.experimental import pallas as pl
from jax.experimental.pallas import tpu as pltpu
from jax.sharding import PartitionSpec as P

ITERS = 2
MESH = pl.DeviceIdType.MESH
HIGH = lax.Precision.HIGHEST
F32 = jnp.float32
BF16 = jnp.bfloat16

S, X, Y, Z, R = 11, 384, 512, 128, 64
WX, WY = 4, 4
NW, NN = 16, 16
XB = X // NW
PARTS = 3
J = 3
NT = (((1,), (1,)), ((), ()))
TN = (((0,), (0,)), ((), ()))


def dot(a, b, dims=(((1,), (0,)), ((), ())), precision=None):
    return lax.dot_general(a, b, dims, precision=precision, preferred_element_type=F32)


def split(v):
    high = v.astype(BF16)
    return high, (v - high.astype(F32)).astype(BF16)


def pairs(size):
    blocks = size // 128
    return [(i, j) for i in range(blocks) for j in range(i, blocks)]


def block(i):
    return slice(i * 128, (i + 1) * 128)


def kernel(
    field, start_x, start_y, start_z,
    core_out, out_x, out_y, out_z,
    fibres, fib_hi, fib_lo, acc_hh, acc_hl,
    shrunk, columns, col_hi, col_lo, second, regrouped,
    part_x, arrive_x, own_x, near_x, mid_x, full_x,
    part_y, arrive_y, own_y, near_y, mid_y, full_y,
    part_z, arrive_z, own_z, near_z, mid_z, full_z,
    gram, begin_x, begin_y, begin_z, basis_x, basis_y, basis_z, elim,
    load_s,
    send_a, recv_a, local_a,
    send_c, recv_c, local_c,
    send_d, recv_d, local_d,
    send_g, recv_g,
):
    w = lax.axis_index("wide")
    n = lax.axis_index("narrow")
    wx, wy = lax.div(w, WY), lax.rem(w, WY)
    nz, nc = lax.div(n, 2), lax.rem(n, 2)
    at_x = [lax.rem(wx + d, WX) for d in range(WX)]
    at_y = [lax.rem(wy + d, WY) for d in range(WY)]
    starts = [
        pltpu.make_async_copy(source, target, load_s.at[i])
        for i, (source, target) in enumerate(
            ((start_x, begin_x), (start_y, begin_y), (start_z, begin_z))
        )
    ]
    for one in starts:
        one.start()

    barrier = pltpu.get_barrier_semaphore()

    def greet(wide, narrow):
        pl.semaphore_signal(barrier, inc=1, device_id=(wide, narrow), device_id_type=MESH)

    @pl.loop(1, NW)
    def _(d):
        greet((w + d) % NW, n)
        greet(w, (n + d) % NN)

    @pl.loop(1, WY)
    def _(dy):
        @pl.loop(1, NN)
        def _(dn):
            greet(wx * WY + (wy + dy) % WY, (n + dn) % NN)

    pl.semaphore_wait(barrier, 2 * (NW - 1) + (WY - 1) * (NN - 1))

    def remote(src, dst, send, recv, wide, narrow):
        return pltpu.make_async_remote_copy(
            src_ref=src, dst_ref=dst, send_sem=send, recv_sem=recv,
            device_id=(wide, narrow), device_id_type=MESH,
        )

    def await_recv(ref, sem):
        remote(ref, ref, sem, sem, w, n).wait_recv()

    def await_send(ref, sem):
        remote(ref, ref, sem, sem, w, n).wait_send()

    mine = pl.ds(w * XB, XB)

    def send_lines(j):
        @pl.loop(0, PARTS)
        def _(q):
            for dx in range(WX):
                for dy in range(WY):
                    if dx or dy:
                        def one(dx=dx, dy=dy):
                            rows = pl.ds(q * (XB // PARTS), XB // PARTS)
                            there = pl.ds(w * XB + q * (XB // PARTS), XB // PARTS)
                            remote(
                                field.at[at_x[dx] + WX * j, rows, at_y[dy]], fibres.at[j, there],
                                send_a, recv_a.at[j], at_x[dx] * WY + at_y[dy], n,
                            ).start()

                        if WX * (j + 1) <= S:
                            one()
                        else:
                            pl.when(at_x[dx] + WX * j < S)(one)

    for j in range(J):
        send_lines(j)

        @pl.when(wx + WX * j < S)
        def _(j=j):
            pltpu.make_async_copy(
                field.at[wx + WX * j, :, wy], fibres.at[j, mine], local_a.at[j]
            ).start()

    for j in range(J):
        @pl.when(wx + WX * j < S)
        def _(j=j):
            pltpu.make_async_copy(
                field.at[wx + WX * j, :, wy], fibres.at[j, mine], local_a.at[j]
            ).wait()
            await_recv(fibres.at[j, pl.ds(0, (NW - 1) * XB)], recv_a.at[j])

        @pl.when(wx + WX * j >= S)
        def _(j=j):
            fibres[j] = jnp.zeros(fibres.shape[1:], F32)

        lines = fibres.at[j].reshape(X * 8, Z)
        for y in range(8):
            high, low = split(lines[pl.ds(y, X, stride=8), :])
            fib_hi[j, :, block(y)] = high
            fib_lo[j, :, block(y)] = low
        high = fib_hi[j]
        hh = dot(high, high, NT)
        hl = dot(high, fib_lo[j], NT)
        acc_hh[:X, :X] = hh if j == 0 else acc_hh[:X, :X] + hh
        acc_hl[:X, :X] = hl if j == 0 else acc_hl[:X, :X] + hl

    def pack(blocks, part):
        for b, (i, j) in enumerate(blocks):
            part[block(b), :] = (
                acc_hh[block(i), block(j)] + acc_hl[block(i), block(j)]
                + acc_hl[block(j), block(i)].T
            )

    def unpack(blocks, full):
        for b, (i, j) in enumerate(blocks):
            one = full[block(b), :]
            gram[block(i), block(j)] = one
            if i != j:
                gram[block(j), block(i)] = one.T

    def all_reduce(mode, size, chunks, tiles, part, arrive, own, near, mid, full):
        rows = tiles * 8
        blocks = pairs(size)

        def spread(chunk):
            if chunks > 1:
                pack(blocks[chunk * tiles :][:tiles], part.at[chunk].reshape(tiles * 128, 128))
            for dx in range(WX):
                for dy in range(WY):
                    if dx or dy:
                        t = at_x[dx] * WY + at_y[dy]
                        remote(
                            part.at[chunk, t], arrive.at[chunk, w],
                            send_g.at[mode, 0], recv_g.at[mode, 0, chunk], t, n,
                        ).start()

        def across(chunk):
            arrive[chunk, w] = part[chunk, w]
            await_recv(arrive.at[chunk, pl.ds(0, NW - 1)], recv_g.at[mode, 0, chunk])
            total = arrive[chunk, 0]
            for t in range(1, NW):
                total = total + arrive[chunk, t]
            own[chunk] = total.reshape(tiles, 8, 128)
            if chunks == 1:
                near[n] = own[0, 0]

                @pl.loop(1, NN)
                def _(d):
                    t = lax.rem(n + d, NN)
                    remote(own.at[0, 0], near.at[n], send_g.at[mode, 1], recv_g.at[mode, 1, 0], w, t).start()
            else:
                @pl.loop(0, tiles)
                def _(t):
                    @pl.when(t + chunk * tiles != n)
                    def _():
                        remote(
                            own.at[chunk, t], near.at[n], send_g.at[mode, 1],
                            recv_g.at[mode, 1, 0], w, t + chunk * tiles,
                        ).start()

        def add_near():
            total = near[0]
            for t in range(1, NN):
                total = total + near[t]
            return total

        def back(chunk):
            if chunks == 1:
                await_recv(near.at[pl.ds(0, NN - 1)], recv_g.at[mode, 1, 0])
                mid[0, 0] = add_near()
            else:
                first = chunk * tiles
                mine_now = (n >= first) & (n < first + tiles)
                tile = n - first

                @pl.when(mine_now)
                def _():
                    near[n] = own[chunk, tile]
                    await_recv(near.at[pl.ds(0, NN - 1)], recv_g.at[mode, 1, 0])
                    mid[chunk, tile] = add_near()

                    @pl.loop(1, NN)
                    def _(d):
                        t = lax.rem(n + d, NN)
                        remote(
                            mid.at[chunk, tile], mid.at[chunk, tile], send_g.at[mode, 2],
                            recv_g.at[mode, 2, chunk], w, t,
                        ).start()

        def share(chunk):
            if chunks > 1:
                first = chunk * tiles
                mine_now = (n >= first) & (n < first + tiles)

                @pl.when(mine_now)
                def _():
                    if tiles > 1:
                        await_recv(mid.at[chunk, pl.ds(0, tiles - 1)], recv_g.at[mode, 2, chunk])

                @pl.when(jnp.logical_not(mine_now))
                def _():
                    await_recv(mid.at[chunk], recv_g.at[mode, 2, chunk])

            for dx in range(WX):
                for dy in range(WY):
                    if dx or dy:
                        remote(
                            mid.at[chunk], full.at[chunk, w], send_g.at[mode, 3],
                            recv_g.at[mode, 3, chunk], at_x[dx] * WY + at_y[dy], n,
                        ).start()
            full[chunk, w] = mid[chunk]

        for stage in (spread, across, back, share):
            for chunk in range(chunks):
                stage(chunk)
        for chunk in range(chunks):
            await_recv(full.at[chunk, pl.ds(0, NW - 1)], recv_g.at[mode, 3, chunk])
            unpack(blocks[chunk * tiles :][:tiles], full.at[chunk].reshape(tiles * 128, 128))

        def drain():
            for chunk in range(chunks):
                await_send(full.at[chunk, pl.ds(0, NW - 1)], send_g.at[mode, 0])
                await_send(full.at[chunk, pl.ds(0, NW - 1)], send_g.at[mode, 3])
            count = chunks * tiles
            if chunks == 1:
                await_send(near.at[pl.ds(0, NN - 1)], send_g.at[mode, 1])
            else:
                @pl.when(n < count)
                def _():
                    await_send(near.at[pl.ds(0, NN - 1)], send_g.at[mode, 2])
                    await_send(near.at[pl.ds(0, count - 1)], send_g.at[mode, 1])

                @pl.when(n >= count)
                def _():
                    await_send(near.at[pl.ds(0, count)], send_g.at[mode, 1])

        return drain

    row_of = lax.broadcasted_iota(jnp.int32, (R, 128), 0)
    line_of = lax.broadcasted_iota(jnp.int32, (8, 128), 0)

    def lower_inverse(inner):
        here = lax.broadcasted_iota(jnp.int32, (R, R), 0)
        there = lax.broadcasted_iota(jnp.int32, (R, R), 1)
        elim[:, :R] = inner
        elim[:, R:] = (here == there).astype(F32)

        def step(b, _):
            start = pl.multiple_of(b * 8, 8)
            whole = elim[...]
            panel = elim[pl.ds(start, 8), :]
            below = row_of >= (b + 1) * 8
            heads = [jnp.broadcast_to(panel[:, i : i + 1], (8, 128)) for i in range(8)]
            lower = [jnp.where(below, whole[:, i : i + 1], 0.0) for i in range(8)]
            for i in range(8):
                scale = lax.rsqrt(heads[i][i : i + 1, :])
                row = panel[i : i + 1, :] * scale
                factor = jnp.where(line_of > i, heads[i] * scale, 0.0)
                under = lower[i] * scale
                for c in range(i + 1, 8):
                    pivot = heads[c][i : i + 1, :] * scale
                    heads[c] = heads[c] - factor * pivot
                    lower[c] = lower[c] - under * pivot
                panel = jnp.where(line_of == i, jnp.broadcast_to(row, (8, 128)), panel - factor * row)
                whole = whole - under * row
            elim[...] = pltpu.roll(whole, 120, 1)
            elim[pl.ds(start, 8), :] = pltpu.roll(panel, 120, 1)
            return 0

        lax.fori_loop(0, R // 8, step, 0)
        return elim[:, :R]

    def subspace(mode, size, begin, basis, out):
        starts[mode].wait()
        basis[...] = begin[...].T

        def turn(_, carry):
            image = dot(gram[:size, :size], basis[...], precision=HIGH)
            inner = dot(image, image, TN, HIGH)
            basis[...] = dot(image, lower_inverse(inner), NT, HIGH)
            return carry

        lax.fori_loop(0, ITERS, turn, 0)
        out[...] = basis[...].T

    drain_x = all_reduce(0, X, 2, 3, part_x, arrive_x, own_x, near_x, mid_x, full_x)
    subspace(0, X, begin_x, basis_x, out_x)

    high, low = split(out_x[...])
    slab = wx * WY
    for j in range(J):
        part = dot(high, fib_hi[j]) + dot(high, fib_lo[j]) + dot(low, fib_hi[j])
        lines = shrunk.at[j].reshape(R * 8, Z)
        for y in range(8):
            lines[pl.ds(y, R, stride=8), :] = part[:, block(y)]

        @pl.when(wx + WX * j < S)
        def _(j=j):
            @pl.loop(0, 8)
            def _(i):
                half = lax.div(i, 2)
                odd = lax.rem(i, 2)
                z = lax.rem(nz + 4 + half + odd - 2 * odd * (half + 1) + 8, 8)
                for dc in range(2):
                    for dy in range(WY):
                        def one(dc=dc, dy=dy):
                            core = lax.rem(nc + dc, 2)
                            t = z * 2 + core
                            remote(
                                shrunk.at[j, t * WY + at_y[dy]], columns.at[j, n * WY + wy], send_c,
                                recv_c.at[j], slab + at_y[dy], t,
                            ).start()

                        if dc or dy:
                            one()
                        else:
                            pl.when(z != nz)(one)

            columns[j, n * WY + wy] = shrunk[j, n * WY + wy]

    for j in range(J):
        @pl.when(wx + WX * j < S)
        def _(j=j):
            await_recv(columns.at[j, pl.ds(0, R - 1)], recv_c.at[j])

        @pl.when(wx + WX * j >= S)
        def _(j=j):
            columns[j] = jnp.zeros(columns.shape[1:], F32)

        high, low = split(columns[j].reshape(Y, Z))
        col_hi[:, block(j)] = high
        col_lo[:, block(j)] = low
    high = col_hi[...]
    acc_hh[...] = dot(high, high, NT)
    acc_hl[...] = dot(high, col_lo[...], NT)
    drain_y = all_reduce(1, Y, 2, 5, part_y, arrive_y, own_y, near_y, mid_y, full_y)
    subspace(1, Y, begin_y, basis_y, out_y)

    row = lax.broadcasted_iota(jnp.int32, (2 * R, R), 0)
    col = lax.broadcasted_iota(jnp.int32, (2 * R, R), 1)
    spread = ((row % 8 < 4) & (row // 8 * 4 + row % 8 == col)).astype(F32)
    high, low = split(dot(spread, out_y[...], precision=HIGH))
    part = dot(high, col_hi[...]) + dot(high, col_lo[...]) + dot(low, col_hi[...])
    total = jnp.zeros((Z, Z), F32)
    for j in range(J):
        one = part[:, block(j)]
        second[j] = one.reshape(NW, 8, Z)
        total = total + dot(one, one, TN, HIGH)
    part_z[...] = total.reshape(1, NW, 8, 128)

    @pl.loop(1, NW)
    def _(d):
        t = (w + d) % NW
        remote(second.at[:, t], regrouped.at[:, w], send_d, recv_d, t, n).start()

    for j in range(J):
        regrouped[j, w] = second[j, w]
    drain_z = all_reduce(2, Z, 1, 1, part_z, arrive_z, own_z, near_z, mid_z, full_z)
    subspace(2, Z, begin_z, basis_z, out_z)

    await_recv(regrouped.at[:, pl.ds(0, NW - 1)], recv_d)
    core_out[...] = dot(regrouped[...].reshape(J * NW * 8, Z), basis_z[...], precision=HIGH)

    drain_x()
    drain_y()
    drain_z()
    await_send(regrouped.at[:, pl.ds(0, NW - 1)], send_d)
    for j in range(J):
        @pl.when(wx + WX * j < S)
        def _(j=j):
            await_send(columns.at[j, pl.ds(0, R - 1)], send_c)
    for j in range(J - 1):
        await_send(fibres.at[j, pl.ds(0, (NW - 1) * XB)], send_a)
    last = WY * (S - WX * (J - 1))

    @pl.when(wx + WX * (J - 1) < S)
    def _():
        await_send(fibres.at[J - 1, pl.ds(0, (last - 1) * XB)], send_a)

    @pl.when(wx + WX * (J - 1) >= S)
    def _():
        await_send(fibres.at[J - 1, pl.ds(0, last * XB)], send_a)


def reduce_scratch(chunks, tiles):
    rows = tiles * 8
    return [
        pltpu.VMEM((chunks, NW, rows, 128), F32),
        pltpu.VMEM((chunks, NW, rows, 128), F32),
        pltpu.VMEM((chunks, tiles, 8, 128), F32),
        pltpu.VMEM((NN, 8, 128), F32),
        pltpu.VMEM((chunks, tiles, 8, 128), F32),
        pltpu.VMEM((chunks, NW, tiles, 8, 128), F32),
    ]


def hand_over(core, fx, fy, fz, core_out, out_x, out_y, out_z):
    core_out[...] = core[...].reshape(WX * J, NN // 4, 8, R)[:S, :, :4, :]
    out_x[...] = fx[...]
    out_y[...] = fy[...]
    out_z[...] = fz[...]


def finish(*arrays):
    vmem = pl.BlockSpec(memory_space=pltpu.VMEM)
    return pl.pallas_call(
        hand_over,
        out_shape=(
            jax.ShapeDtypeStruct((S, NN // 4, 4, R), F32),
            jax.ShapeDtypeStruct((R, X), F32),
            jax.ShapeDtypeStruct((R, Y), F32),
            jax.ShapeDtypeStruct((R, Z), F32),
        ),
        in_specs=[vmem] * 4,
    )(*arrays)


def body(field, start_x, start_y, start_z):
    vmem = pl.BlockSpec(memory_space=pltpu.VMEM)
    dma = pltpu.SemaphoreType.DMA
    core, fx, fy, fz = pl.pallas_call(
        kernel,
        out_shape=(
            jax.ShapeDtypeStruct((J * NW * 8, R), F32),
            jax.ShapeDtypeStruct((R, X), F32),
            jax.ShapeDtypeStruct((R, Y), F32),
            jax.ShapeDtypeStruct((R, Z), F32),
        ),
        in_specs=[pl.BlockSpec(memory_space=pl.ANY)] * 4,
        out_specs=(vmem,) * 4,
        scratch_shapes=[
            pltpu.VMEM((J, X, 8, Z), F32),
            pltpu.VMEM((J, X, 8 * Z), BF16),
            pltpu.VMEM((J, X, 8 * Z), BF16),
            pltpu.VMEM((Y, Y), F32),
            pltpu.VMEM((Y, Y), F32),
            pltpu.VMEM((J, R, 8, Z), F32),
            pltpu.VMEM((J, R, 8, Z), F32),
            pltpu.VMEM((Y, J * Z), BF16),
            pltpu.VMEM((Y, J * Z), BF16),
            pltpu.VMEM((J, NW, 8, Z), F32),
            pltpu.VMEM((J, NW, 8, Z), F32),
            *reduce_scratch(2, 3),
            *reduce_scratch(2, 5),
            *reduce_scratch(1, 1),
            pltpu.VMEM((Y, Y), F32),
            pltpu.VMEM((R, X), F32),
            pltpu.VMEM((R, Y), F32),
            pltpu.VMEM((R, Z), F32),
            pltpu.VMEM((X, R), F32),
            pltpu.VMEM((Y, R), F32),
            pltpu.VMEM((Z, R), F32),
            pltpu.VMEM((R, 128), F32),
            dma((3,)),
            dma, dma((J,)), dma((J,)),
            dma, dma((J,)), dma,
            dma, dma, dma,
            dma((3, 4)), dma((3, 4, 2)),
        ],
        compiler_params=pltpu.CompilerParams(collective_id=0, has_side_effects=True),
    )(field.reshape(S, XB, WY, 8, Z), start_x.T, start_y.T, start_z.T)
    core, fx, fy, fz = finish(core, fx, fy, fz)
    return core, fx.T, fy.T, fz.T


def solution(mesh):
    return jax.shard_map(
        body,
        mesh=mesh,
        in_specs=(P(None, "wide", "narrow", None), P(), P(), P()),
        out_specs=(P(None, "narrow", "wide", None), P(), P(), P()),
        check_vma=False,
    )
```

time: 231 us -> 184 us (0.80)
  Pallas kernels: 219 us -> 183 us
  local copies, waits for them, and re-layouts: 11.4 us -> 0 us
    pallas_call x1, Pallas kernels: 219 us -> 181 us  [body(): pl.pallas_call(kernel, out_shape=(jax.ShapeDtypeStruct((J * NW * 8, R), F...]
    unnamed x6 -> x0, local copies, waits for them, and re-layouts: 9.86 us -> none
where the time goes in v2:
time: 184 us; the launch traced here: 183 us
  Pallas kernels  183 us (99%)
    pallas_call x1, Pallas kernels, body(): pl.pallas_call(kernel, out_shape=(jax.ShapeDtypeStruct((J * NW * 8, R), F...  181 us

profile of v2, /device:TPU:1, one launch (start us, length us, event | category | flops | bytes accessed | tf_op | source)
XLA Modules:
  0.0 183.5 jit_solution(7849903210072620359)
XLA Ops:
  0.6 181.1 %shard_map.75 = (f32[384,64]{1,0:T(8,128)}, f32[64,384]{1,0:T(8,128)}, f32[64,512]{1,0:T(8,128)}, f32[64,128]{1,0:T(8,128)}) custom-call(f32[11,24,4,8,128]{4,3,2,1,0:T(8,128)} %bitcast.7, f32[64,384]{1,0:T(8,128)} %bitcast.9, f32[64,512]{1,0:T(8,128)} %bitcast.8, f32[64,128]{1,0:T(8,128)} %bitcast.10), custom_call_target="tpu_custom_call" | custom-call | tf_op jit(solution)/shard_map/pallas_call | solution.py:471
  181.7 1.8 shard_map.76

commit v3 on v2

--- a/solution.py
+++ b/solution.py
@@ -46,8 +46,8 @@
     core_out, out_x, out_y, out_z,
     fibres, fib_hi, fib_lo, acc_hh, acc_hl,
     shrunk, columns, col_hi, col_lo, second, regrouped,
-    part_x, arrive_x, own_x, near_x, mid_x, full_x,
-    part_y, arrive_y, own_y, near_y, mid_y, full_y,
+    part_x, pair_x, arrive_x, own_x, near_x, mid_x, full_x,
+    part_y, pair_y, arrive_y, own_y, near_y, mid_y, full_y,
     part_z, arrive_z, own_z, near_z, mid_z, full_z,
     gram, begin_x, begin_y, begin_z, basis_x, basis_y, basis_z, elim,
     load_s,
@@ -154,135 +154,118 @@
         acc_hh[:X, :X] = hh if j == 0 else acc_hh[:X, :X] + hh
         acc_hl[:X, :X] = hl if j == 0 else acc_hl[:X, :X] + hl
 
-    def pack(blocks, part):
-        for b, (i, j) in enumerate(blocks):
-            part[block(b), :] = (
-                acc_hh[block(i), block(j)] + acc_hl[block(i), block(j)]
-                + acc_hl[block(j), block(i)].T
-            )
-
-    def unpack(blocks, full):
-        for b, (i, j) in enumerate(blocks):
-            one = full[block(b), :]
-            gram[block(i), block(j)] = one
-            if i != j:
-                gram[block(j), block(i)] = one.T
-
-    def all_reduce(mode, size, chunks, tiles, part, arrive, own, near, mid, full):
-        rows = tiles * 8
-        blocks = pairs(size)
-
-        def spread(chunk):
-            if chunks > 1:
-                pack(blocks[chunk * tiles :][:tiles], part.at[chunk].reshape(tiles * 128, 128))
-            for dx in range(WX):
-                for dy in range(WY):
-                    if dx or dy:
-                        t = at_x[dx] * WY + at_y[dy]
-                        remote(
-                            part.at[chunk, t], arrive.at[chunk, w],
-                            send_g.at[mode, 0], recv_g.at[mode, 0, chunk], t, n,
-                        ).start()
-
-        def across(chunk):
-            arrive[chunk, w] = part[chunk, w]
-            await_recv(arrive.at[chunk, pl.ds(0, NW - 1)], recv_g.at[mode, 0, chunk])
-            total = arrive[chunk, 0]
+    def pack(i, j):
+        return (
+            acc_hh[block(i), block(j)] + acc_hl[block(i), block(j)]
+            + acc_hl[block(j), block(i)].T
+        ).reshape(NW, 8, 128)
+
+    def unpack(i, j, one):
+        one = one.reshape(128, 128)
+        gram[block(i), block(j)] = one
+        if i != j:
+            gram[block(j), block(i)] = one.T
+
+    def to_wide(source, target, send, recv):
+        for dx in range(WX):
+            for dy in range(WY):
+                if dx or dy:
+                    t = at_x[dx] * WY + at_y[dy]
+                    remote(source(t), target, send, recv, t, n).start()
+
+    partner = nz * 2 + 1 - nc
+
+    def all_reduce(mode, size, cuts, part, pair, arrive, own, near, mid, full):
+        places = pairs(size)
+        half = len(places) // 2
+        chunks = [(a, b - a) for a, b in zip((0, *cuts), (*cuts, half))]
+        sends = [send_g.at[mode, stage] for stage in range(5)]
+
+        def swap(c, first, count):
+            for h in range(2):
+                for k in range(first, first + count):
+                    part[h, k] = pack(*places[h * half + k])
+            here = pl.ds(first, count)
+            remote(part.at[1 - nc, here], pair.at[here], sends[0], recv_g.at[mode, 0, c], w, partner).start()
+
+        def spread(c, first, count):
+            here = pl.ds(first, count)
+            await_recv(pair.at[here], recv_g.at[mode, 0, c])
+            pair[here] = part[nc, here] + pair[here]
+            to_wide(lambda t: pair.at[here, t], arrive.at[here, w], sends[1], recv_g.at[mode, 1, c])
+            arrive[here, w] = pair[here, w]
+
+        def across(c, first, count):
+            here = pl.ds(first, count)
+            await_recv(arrive.at[here, pl.ds(0, NW - 1)], recv_g.at[mode, 1, c])
+            total = arrive[here, 0]
             for t in range(1, NW):
-                total = total + arrive[chunk, t]
-            own[chunk] = total.reshape(tiles, 8, 128)
-            if chunks == 1:
-                near[n] = own[0, 0]
-
-                @pl.loop(1, NN)
-                def _(d):
-                    t = lax.rem(n + d, NN)
-                    remote(own.at[0, 0], near.at[n], send_g.at[mode, 1], recv_g.at[mode, 1, 0], w, t).start()
-            else:
-                @pl.loop(0, tiles)
-                def _(t):
-                    @pl.when(t + chunk * tiles != n)
-                    def _():
-                        remote(
-                            own.at[chunk, t], near.at[n], send_g.at[mode, 1],
-                            recv_g.at[mode, 1, 0], w, t + chunk * tiles,
-                        ).start()
-
-        def add_near():
-            total = near[0]
-            for t in range(1, NN):
-                total = total + near[t]
-            return total
-
-        def back(chunk):
-            if chunks == 1:
-                await_recv(near.at[pl.ds(0, NN - 1)], recv_g.at[mode, 1, 0])
-                mid[0, 0] = add_near()
-            else:
-                first = chunk * tiles
-                mine_now = (n >= first) & (n < first + tiles)
-                tile = n - first
-
-                @pl.when(mine_now)
-                def _():
-                    near[n] = own[chunk, tile]
-                    await_recv(near.at[pl.ds(0, NN - 1)], recv_g.at[mode, 1, 0])
-                    mid[chunk, tile] = add_near()
-
-                    @pl.loop(1, NN)
-                    def _(d):
-                        t = lax.rem(n + d, NN)
-                        remote(
-                            mid.at[chunk, tile], mid.at[chunk, tile], send_g.at[mode, 2],
-                            recv_g.at[mode, 2, chunk], w, t,
-                        ).start()
-
-        def share(chunk):
-            if chunks > 1:
-                first = chunk * tiles
-                mine_now = (n >= first) & (n < first + tiles)
-
-                @pl.when(mine_now)
-                def _():
-                    if tiles > 1:
-                        await_recv(mid.at[chunk, pl.ds(0, tiles - 1)], recv_g.at[mode, 2, chunk])
-
-                @pl.when(jnp.logical_not(mine_now))
-                def _():
-                    await_recv(mid.at[chunk], recv_g.at[mode, 2, chunk])
-
-            for dx in range(WX):
-                for dy in range(WY):
-                    if dx or dy:
-                        remote(
-                            mid.at[chunk], full.at[chunk, w], send_g.at[mode, 3],
-                            recv_g.at[mode, 3, chunk], at_x[dx] * WY + at_y[dy], n,
-                        ).start()
-            full[chunk, w] = mid[chunk]
-
-        for stage in (spread, across, back, share):
-            for chunk in range(chunks):
-                stage(chunk)
-        for chunk in range(chunks):
-            await_recv(full.at[chunk, pl.ds(0, NW - 1)], recv_g.at[mode, 3, chunk])
-            unpack(blocks[chunk * tiles :][:tiles], full.at[chunk].reshape(tiles * 128, 128))
+                total = total + arrive[here, t]
+            own[here] = total
+            for d in (1, 7, 2, 6, 3, 5, 4):
+                t = lax.rem(nz + d, 8) * 2 + nc
+                remote(own.at[here], near.at[nz, here], sends[2], recv_g.at[mode, 2, c], w, t).start()
+            near[nz, here] = total
+
+        def back(c, first, count):
+            here = pl.ds(first, count)
+            await_recv(near.at[pl.ds(0, 7), here], recv_g.at[mode, 2, c])
+            total = near[0, here]
+            for t in range(1, 8):
+                total = total + near[t, here]
+            mid[here] = total
+            to_wide(lambda t: mid.at[here], full.at[nc, here, w], sends[3], recv_g.at[mode, 3, c])
+            full[nc, here, w] = total
+
+        def share(c, first, count):
+            here = pl.ds(first, count)
+            await_recv(full.at[nc, here, pl.ds(0, NW - 1)], recv_g.at[mode, 3, c])
+            remote(full.at[nc, here], full.at[nc, here], sends[4], recv_g.at[mode, 4, c], w, partner).start()
+
+        def finish(c, first, count):
+            here = pl.ds(first, count)
+            await_recv(full.at[1 - nc, here], recv_g.at[mode, 4, c])
+            for h in range(2):
+                for k in range(first, first + count):
+                    unpack(*places[h * half + k], full[h, k])
+
+        for stage in (swap, spread, across, back, share, finish):
+            for c, chunk in enumerate(chunks):
+                stage(c, *chunk)
 
         def drain():
-            for chunk in range(chunks):
-                await_send(full.at[chunk, pl.ds(0, NW - 1)], send_g.at[mode, 0])
-                await_send(full.at[chunk, pl.ds(0, NW - 1)], send_g.at[mode, 3])
-            count = chunks * tiles
-            if chunks == 1:
-                await_send(near.at[pl.ds(0, NN - 1)], send_g.at[mode, 1])
-            else:
-                @pl.when(n < count)
-                def _():
-                    await_send(near.at[pl.ds(0, NN - 1)], send_g.at[mode, 2])
-                    await_send(near.at[pl.ds(0, count - 1)], send_g.at[mode, 1])
-
-                @pl.when(n >= count)
-                def _():
-                    await_send(near.at[pl.ds(0, count)], send_g.at[mode, 1])
+            await_send(pair, sends[0])
+            await_send(arrive.at[:, pl.ds(0, NW - 1)], sends[1])
+            await_send(near.at[pl.ds(0, 7)], sends[2])
+            await_send(arrive.at[:, pl.ds(0, NW - 1)], sends[3])
+            await_send(pair, sends[4])
+
+        return drain
+
+    def all_reduce_small(mode, part, arrive, own, near, mid, full):
+        to_wide(lambda t: part.at[t], arrive.at[w], send_g.at[mode, 0], recv_g.at[mode, 0, 0])
+        arrive[w] = part[w]
+        await_recv(arrive.at[pl.ds(0, NW - 1)], recv_g.at[mode, 0, 0])
+        total = arrive[0]
+        for t in range(1, NW):
+            total = total + arrive[t]
+        own[...] = total
+        for d in (2, 15, 3, 14, 4, 13, 5, 12, 6, 11, 7, 10, 8, 9, 1):
+            t = lax.rem(n + d, NN)
+            remote(own, near.at[n], send_g.at[mode, 1], recv_g.at[mode, 1, 0], w, t).start()
+        near[n] = total
+        await_recv(near.at[pl.ds(0, NN - 1)], recv_g.at[mode, 1, 0])
+        total = near[0]
+        for t in range(1, NN):
+            total = total + near[t]
+        mid[...] = total
+        to_wide(lambda t: mid, full.at[w], send_g.at[mode, 2], recv_g.at[mode, 2, 0])
+        full[w] = total
+        await_recv(full.at[pl.ds(0, NW - 1)], recv_g.at[mode, 2, 0])
+
+        def drain():
+            for stage in range(3):
+                await_send(full.at[pl.ds(0, NW - 1)], send_g.at[mode, stage])
 
         return drain
 
@@ -333,7 +316,7 @@
         lax.fori_loop(0, ITERS, turn, 0)
         out[...] = basis[...].T
 
-    drain_x = all_reduce(0, X, 2, 3, part_x, arrive_x, own_x, near_x, mid_x, full_x)
+    drain_x = all_reduce(0, X, (2,), part_x, pair_x, arrive_x, own_x, near_x, mid_x, full_x)
     subspace(0, X, begin_x, basis_x, out_x)
 
     high, low = split(out_x[...])
@@ -383,7 +366,7 @@
     high = col_hi[...]
     acc_hh[...] = dot(high, high, NT)
     acc_hl[...] = dot(high, col_lo[...], NT)
-    drain_y = all_reduce(1, Y, 2, 5, part_y, arrive_y, own_y, near_y, mid_y, full_y)
+    drain_y = all_reduce(1, Y, (3,), part_y, pair_y, arrive_y, own_y, near_y, mid_y, full_y)
     subspace(1, Y, begin_y, basis_y, out_y)
 
     row = lax.broadcasted_iota(jnp.int32, (2 * R, R), 0)
@@ -396,7 +379,7 @@
         one = part[:, block(j)]
         second[j] = one.reshape(NW, 8, Z)
         total = total + dot(one, one, TN, HIGH)
-    part_z[...] = total.reshape(1, NW, 8, 128)
+    part_z[...] = total.reshape(NW, 8, 128)
 
     @pl.loop(1, NW)
     def _(d):
@@ -405,7 +388,8 @@
 
     for j in range(J):
         regrouped[j, w] = second[j, w]
-    drain_z = all_reduce(2, Z, 1, 1, part_z, arrive_z, own_z, near_z, mid_z, full_z)
+    drain_z = all_reduce_small(2, part_z, arrive_z, own_z, near_z, mid_z, full_z)
+    gram[:Z, :Z] = full_z[...].reshape(Z, Z)
     subspace(2, Z, begin_z, basis_z, out_z)
 
     await_recv(regrouped.at[:, pl.ds(0, NW - 1)], recv_d)
@@ -432,15 +416,15 @@
         await_send(fibres.at[J - 1, pl.ds(0, last * XB)], send_a)
 
 
-def reduce_scratch(chunks, tiles):
-    rows = tiles * 8
+def reduce_scratch(half):
     return [
-        pltpu.VMEM((chunks, NW, rows, 128), F32),
-        pltpu.VMEM((chunks, NW, rows, 128), F32),
-        pltpu.VMEM((chunks, tiles, 8, 128), F32),
-        pltpu.VMEM((NN, 8, 128), F32),
-        pltpu.VMEM((chunks, tiles, 8, 128), F32),
-        pltpu.VMEM((chunks, NW, tiles, 8, 128), F32),
+        pltpu.VMEM((2, half, NW, 8, 128), F32),
+        pltpu.VMEM((half, NW, 8, 128), F32),
+        pltpu.VMEM((half, NW, 8, 128), F32),
+        pltpu.VMEM((half, 8, 128), F32),
+        pltpu.VMEM((8, half, 8, 128), F32),
+        pltpu.VMEM((half, 8, 128), F32),
+        pltpu.VMEM((2, half, NW, 8, 128), F32),
     ]
 
 
@@ -490,9 +474,14 @@
             pltpu.VMEM((Y, J * Z), BF16),
             pltpu.VMEM((J, NW, 8, Z), F32),
             pltpu.VMEM((J, NW, 8, Z), F32),
-            *reduce_scratch(2, 3),
-            *reduce_scratch(2, 5),
-            *reduce_scratch(1, 1),
+            *reduce_scratch(3),
+            *reduce_scratch(5),
+            pltpu.VMEM((NW, 8, 128), F32),
+            pltpu.VMEM((NW, 8, 128), F32),
+            pltpu.VMEM((8, 128), F32),
+            pltpu.VMEM((NN, 8, 128), F32),
+            pltpu.VMEM((8, 128), F32),
+            pltpu.VMEM((NW, 8, 128), F32),
             pltpu.VMEM((Y, Y), F32),
             pltpu.VMEM((R, X), F32),
             pltpu.VMEM((R, Y), F32),
@@ -505,7 +494,7 @@
             dma, dma((J,)), dma((J,)),
             dma, dma((J,)), dma,
             dma, dma, dma,
-            dma((3, 4)), dma((3, 4, 2)),
+            dma((3, 5)), dma((3, 5, 2)),
         ],
         compiler_params=pltpu.CompilerParams(collective_id=0, has_side_effects=True),
     )(field.reshape(S, XB, WY, 8, Z), start_x.T, start_y.T, start_z.T)

time: 184 us -> 174 us (0.946)
  Pallas kernels: 183 us -> 173 us
    pallas_call x1, Pallas kernels: 181 us -> 171 us  [body(): pl.pallas_call(kernel, out_shape=(jax.ShapeDtypeStruct((J * NW * 8, R), F...]
where the time goes in v3:
time: 174 us; the launch traced here: 173 us
  Pallas kernels  173 us (99%)
    pallas_call x1, Pallas kernels, body(): pl.pallas_call(kernel, out_shape=(jax.ShapeDtypeStruct((J * NW * 8, R), F...  171 us

profile of v3, /device:TPU:1, one launch (start us, length us, event | category | flops | bytes accessed | tf_op | source)
XLA Modules:
  0.0 173.4 jit_solution(10193921918564653387)
XLA Ops:
  0.6 171.0 %shard_map.75 = (f32[384,64]{1,0:T(8,128)}, f32[64,384]{1,0:T(8,128)}, f32[64,512]{1,0:T(8,128)}, f32[64,128]{1,0:T(8,128)}) custom-call(f32[11,24,4,8,128]{4,3,2,1,0:T(8,128)} %bitcast.7, f32[64,384]{1,0:T(8,128)} %bitcast.9, f32[64,512]{1,0:T(8,128)} %bitcast.8, f32[64,128]{1,0:T(8,128)} %bitcast.10), custom_call_target="tpu_custom_call" | custom-call | tf_op jit(solution)/shard_map/pallas_call | solution.py:455
  171.6 1.8 %shard_map.76 = (f32[11,4,4,64]{3,2,1,0:T(4,128)}, f32[64,384]{1,0:T(8,128)}, f32[64,512]{1,0:T(8,128)}, f32[64,128]{1,0:T(8,128)}) custom-call(f32[384,64]{1,0:T(8,128)} %get-tuple-element.12.core, f32[64,384]{1,0:T(8,128)} %get-tuple-element.13.fx, f32[64,512]{1,0:T(8,128)} %get-tuple-element.14.fy, f32[64,128]{1,0:T(8,128)} %get-tuple-element.15.fz), custom_call_target="tpu_custom_call" | custom-call | tf_op jit(solution)/shard_map/pallas_call | solution.py:440

commit v4 on v3

--- a/solution.py
+++ b/solution.py
@@ -49,7 +49,7 @@
     part_x, pair_x, arrive_x, own_x, near_x, mid_x, full_x,
     part_y, pair_y, arrive_y, own_y, near_y, mid_y, full_y,
     part_z, arrive_z, own_z, near_z, mid_z, full_z,
-    gram, begin_x, begin_y, begin_z, basis_x, basis_y, basis_z, elim,
+    gram, begin_x, begin_y, begin_z, elim,
     load_s,
     send_a, recv_a, local_a,
     send_c, recv_c, local_c,
@@ -78,16 +78,10 @@
 
     @pl.loop(1, NW)
     def _(d):
-        greet((w + d) % NW, n)
-        greet(w, (n + d) % NN)
-
-    @pl.loop(1, WY)
-    def _(dy):
-        @pl.loop(1, NN)
-        def _(dn):
-            greet(wx * WY + (wy + dy) % WY, (n + dn) % NN)
-
-    pl.semaphore_wait(barrier, 2 * (NW - 1) + (WY - 1) * (NN - 1))
+        greet(lax.rem(w + d, NW), n)
+        greet(w, lax.rem(n + d, NN))
+
+    pl.semaphore_wait(barrier, NW + NN - 2)
 
     def remote(src, dst, send, recv, wide, narrow):
         return pltpu.make_async_remote_copy(
@@ -269,7 +263,6 @@
 
         return drain
 
-    row_of = lax.broadcasted_iota(jnp.int32, (R, 128), 0)
     line_of = lax.broadcasted_iota(jnp.int32, (8, 128), 0)
 
     def lower_inverse(inner):
@@ -277,47 +270,45 @@
         there = lax.broadcasted_iota(jnp.int32, (R, R), 1)
         elim[:, :R] = inner
         elim[:, R:] = (here == there).astype(F32)
-
-        def step(b, _):
-            start = pl.multiple_of(b * 8, 8)
-            whole = elim[...]
-            panel = elim[pl.ds(start, 8), :]
-            below = row_of >= (b + 1) * 8
-            heads = [jnp.broadcast_to(panel[:, i : i + 1], (8, 128)) for i in range(8)]
-            lower = [jnp.where(below, whole[:, i : i + 1], 0.0) for i in range(8)]
+        groups = [pl.ds(8 * g, 8) for g in range(R // 8)]
+        for g, group in enumerate(groups):
+            lanes = [slice(8 * g + i, 8 * g + i + 1) for i in range(8)]
+            panel = elim[group, :]
+            heads = [jnp.broadcast_to(panel[:, lane], (8, 128)) for lane in lanes]
+            below = [elim[other, :] for other in groups[g + 1 :]]
+            lower = [[jnp.broadcast_to(one[:, lane], (8, 128)) for lane in lanes] for one in below]
             for i in range(8):
                 scale = lax.rsqrt(heads[i][i : i + 1, :])
                 row = panel[i : i + 1, :] * scale
                 factor = jnp.where(line_of > i, heads[i] * scale, 0.0)
-                under = lower[i] * scale
-                for c in range(i + 1, 8):
-                    pivot = heads[c][i : i + 1, :] * scale
+                pivots = {c: heads[c][i : i + 1, :] * scale for c in range(i + 1, 8)}
+                for c, pivot in pivots.items():
                     heads[c] = heads[c] - factor * pivot
-                    lower[c] = lower[c] - under * pivot
                 panel = jnp.where(line_of == i, jnp.broadcast_to(row, (8, 128)), panel - factor * row)
-                whole = whole - under * row
-            elim[...] = pltpu.roll(whole, 120, 1)
-            elim[pl.ds(start, 8), :] = pltpu.roll(panel, 120, 1)
-            return 0
-
-        lax.fori_loop(0, R // 8, step, 0)
-        return elim[:, :R]
-
-    def subspace(mode, size, begin, basis, out):
+                for q in range(len(below)):
+                    under = lower[q][i] * scale
+                    for c, pivot in pivots.items():
+                        lower[q][c] = lower[q][c] - under * pivot
+                    below[q] = below[q] - under * row
+            elim[group, :] = panel
+            for other, one in zip(groups[g + 1 :], below):
+                elim[other, :] = one
+        return elim[:, R:]
+
+    def subspace(mode, size, begin, basis):
         starts[mode].wait()
-        basis[...] = begin[...].T
+        basis[...] = begin[...]
 
         def turn(_, carry):
-            image = dot(gram[:size, :size], basis[...], precision=HIGH)
-            inner = dot(image, image, TN, HIGH)
-            basis[...] = dot(image, lower_inverse(inner), NT, HIGH)
+            image = dot(basis[...], gram[:size, :size], precision=HIGH)
+            inner = dot(image, image, NT, HIGH)
+            basis[...] = dot(lower_inverse(inner), image, precision=HIGH)
             return carry
 
         lax.fori_loop(0, ITERS, turn, 0)
-        out[...] = basis[...].T
-
-    drain_x = all_reduce(0, X, (2,), part_x, pair_x, arrive_x, own_x, near_x, mid_x, full_x)
-    subspace(0, X, begin_x, basis_x, out_x)
+
+    drain_x = all_reduce(0, X, (1,), part_x, pair_x, arrive_x, own_x, near_x, mid_x, full_x)
+    subspace(0, X, begin_x, out_x)
 
     high, low = split(out_x[...])
     slab = wx * WY
@@ -366,8 +357,8 @@
     high = col_hi[...]
     acc_hh[...] = dot(high, high, NT)
     acc_hl[...] = dot(high, col_lo[...], NT)
-    drain_y = all_reduce(1, Y, (3,), part_y, pair_y, arrive_y, own_y, near_y, mid_y, full_y)
-    subspace(1, Y, begin_y, basis_y, out_y)
+    drain_y = all_reduce(1, Y, (2,), part_y, pair_y, arrive_y, own_y, near_y, mid_y, full_y)
+    subspace(1, Y, begin_y, out_y)
 
     row = lax.broadcasted_iota(jnp.int32, (2 * R, R), 0)
     col = lax.broadcasted_iota(jnp.int32, (2 * R, R), 1)
@@ -390,10 +381,10 @@
         regrouped[j, w] = second[j, w]
     drain_z = all_reduce_small(2, part_z, arrive_z, own_z, near_z, mid_z, full_z)
     gram[:Z, :Z] = full_z[...].reshape(Z, Z)
-    subspace(2, Z, begin_z, basis_z, out_z)
+    subspace(2, Z, begin_z, out_z)
 
     await_recv(regrouped.at[:, pl.ds(0, NW - 1)], recv_d)
-    core_out[...] = dot(regrouped[...].reshape(J * NW * 8, Z), basis_z[...], precision=HIGH)
+    core_out[...] = dot(regrouped[...].reshape(J * NW * 8, Z), out_z[...], NT, HIGH)
 
     drain_x()
     drain_y()
@@ -486,9 +477,6 @@
             pltpu.VMEM((R, X), F32),
             pltpu.VMEM((R, Y), F32),
             pltpu.VMEM((R, Z), F32),
-            pltpu.VMEM((X, R), F32),
-            pltpu.VMEM((Y, R), F32),
-            pltpu.VMEM((Z, R), F32),
             pltpu.VMEM((R, 128), F32),
             dma((3,)),
             dma, dma((J,)), dma((J,)),

time: 174 us -> 163 us (0.937)
  Pallas kernels: 173 us -> 162 us
    pallas_call x1, Pallas kernels: 171 us -> 160 us  [body(): pl.pallas_call(kernel, out_shape=(jax.ShapeDtypeStruct((J * NW * 8, R), F...]
where the time goes in v4:
time: 163 us
  Pallas kernels  162 us (99%)
    pallas_call x1, Pallas kernels, body(): pl.pallas_call(kernel, out_shape=(jax.ShapeDtypeStruct((J * NW * 8, R), F...  160 us

profile of v4, /device:TPU:1, one launch (start us, length us, event | category | flops | bytes accessed | tf_op | source)
XLA Modules:
  0.0 162.5 jit_solution(4921393044322830822)
XLA Ops:
  0.6 160.1 %shard_map.75 = (f32[384,64]{1,0:T(8,128)}, f32[64,384]{1,0:T(8,128)}, f32[64,512]{1,0:T(8,128)}, f32[64,128]{1,0:T(8,128)}) custom-call(f32[11,24,4,8,128]{4,3,2,1,0:T(8,128)} %bitcast.7, f32[64,384]{1,0:T(8,128)} %bitcast.9, f32[64,512]{1,0:T(8,128)} %bitcast.8, f32[64,128]{1,0:T(8,128)} %bitcast.10), custom_call_target="tpu_custom_call" | custom-call | tf_op jit(solution)/shard_map/pallas_call | solution.py:446
  160.8 1.8 %shard_map.76 = (f32[11,4,4,64]{3,2,1,0:T(4,128)}, f32[64,384]{1,0:T(8,128)}, f32[64,512]{1,0:T(8,128)}, f32[64,128]{1,0:T(8,128)}) custom-call(f32[384,64]{1,0:T(8,128)} %get-tuple-element.12.core, f32[64,384]{1,0:T(8,128)} %get-tuple-element.13.fx, f32[64,512]{1,0:T(8,128)} %get-tuple-element.14.fy, f32[64,128]{1,0:T(8,128)} %get-tuple-element.15.fz), custom_call_target="tpu_custom_call" | custom-call | tf_op jit(solution)/shard_map/pallas_call | solution.py:431

commit v5 on v4

--- a/solution.py
+++ b/solution.py
@@ -49,8 +49,8 @@
     part_x, pair_x, arrive_x, own_x, near_x, mid_x, full_x,
     part_y, pair_y, arrive_y, own_y, near_y, mid_y, full_y,
     part_z, arrive_z, own_z, near_z, mid_z, full_z,
-    gram, begin_x, begin_y, begin_z, elim,
-    load_s,
+    gram_hi, gram_lo, begin_x, begin_y, begin_z, elim,
+    load_s, load_f, held,
     send_a, recv_a, local_a,
     send_c, recv_c, local_c,
     send_d, recv_d, local_d,
@@ -71,6 +71,12 @@
     for one in starts:
         one.start()
 
+    stages = []
+    for j in range(J):
+        some = pl.ds(WX * j, min(WX, S - WX * j))
+        stages.append(pltpu.make_async_copy(field.at[some], held.at[some], load_f.at[j]))
+        stages[j].start()
+
     barrier = pltpu.get_barrier_semaphore()
 
     def greet(wide, narrow):
@@ -107,7 +113,7 @@
                             rows = pl.ds(q * (XB // PARTS), XB // PARTS)
                             there = pl.ds(w * XB + q * (XB // PARTS), XB // PARTS)
                             remote(
-                                field.at[at_x[dx] + WX * j, rows, at_y[dy]], fibres.at[j, there],
+                                held.at[at_x[dx] + WX * j, rows, at_y[dy]], fibres.at[j, there],
                                 send_a, recv_a.at[j], at_x[dx] * WY + at_y[dy], n,
                             ).start()
 
@@ -117,19 +123,20 @@
                             pl.when(at_x[dx] + WX * j < S)(one)
 
     for j in range(J):
+        stages[j].wait()
         send_lines(j)
 
         @pl.when(wx + WX * j < S)
         def _(j=j):
             pltpu.make_async_copy(
-                field.at[wx + WX * j, :, wy], fibres.at[j, mine], local_a.at[j]
+                held.at[wx + WX * j, :, wy], fibres.at[j, mine], local_a.at[j]
             ).start()
 
     for j in range(J):
         @pl.when(wx + WX * j < S)
         def _(j=j):
             pltpu.make_async_copy(
-                field.at[wx + WX * j, :, wy], fibres.at[j, mine], local_a.at[j]
+                held.at[wx + WX * j, :, wy], fibres.at[j, mine], local_a.at[j]
             ).wait()
             await_recv(fibres.at[j, pl.ds(0, (NW - 1) * XB)], recv_a.at[j])
 
@@ -156,9 +163,8 @@
 
     def unpack(i, j, one):
         one = one.reshape(128, 128)
-        gram[block(i), block(j)] = one
-        if i != j:
-            gram[block(j), block(i)] = one.T
+        for here, there, values in ((i, j, one), (j, i, one.T))[: 1 + (i != j)]:
+            gram_hi[block(here), block(there)], gram_lo[block(here), block(there)] = split(values)
 
     def to_wide(source, target, send, recv):
         for dx in range(WX):
@@ -300,7 +306,9 @@
         basis[...] = begin[...]
 
         def turn(_, carry):
-            image = dot(basis[...], gram[:size, :size], precision=HIGH)
+            high, low = split(basis[...])
+            both = dot(jnp.concatenate([high, low], axis=0), gram_hi[:size, :size])
+            image = both[:R] + both[R:] + dot(high, gram_lo[:size, :size])
             inner = dot(image, image, NT, HIGH)
             basis[...] = dot(lower_inverse(inner), image, precision=HIGH)
             return carry
@@ -380,7 +388,7 @@
     for j in range(J):
         regrouped[j, w] = second[j, w]
     drain_z = all_reduce_small(2, part_z, arrive_z, own_z, near_z, mid_z, full_z)
-    gram[:Z, :Z] = full_z[...].reshape(Z, Z)
+    unpack(0, 0, full_z[...])
     subspace(2, Z, begin_z, out_z)
 
     await_recv(regrouped.at[:, pl.ds(0, NW - 1)], recv_d)
@@ -473,12 +481,15 @@
             pltpu.VMEM((NN, 8, 128), F32),
             pltpu.VMEM((8, 128), F32),
             pltpu.VMEM((NW, 8, 128), F32),
-            pltpu.VMEM((Y, Y), F32),
+            pltpu.VMEM((Y, Y), BF16),
+            pltpu.VMEM((Y, Y), BF16),
             pltpu.VMEM((R, X), F32),
             pltpu.VMEM((R, Y), F32),
             pltpu.VMEM((R, Z), F32),
             pltpu.VMEM((R, 128), F32),
             dma((3,)),
+            dma((J,)),
+            pltpu.VMEM((S, XB, WY, 8, Z), F32),
             dma, dma((J,)), dma((J,)),
             dma, dma((J,)), dma,
             dma, dma, dma,

time: 163 us -> 161 us (0.988)
  Pallas kernels: 162 us -> 160 us
    pallas_call x1, Pallas kernels: 160 us -> 158 us  [body(): pl.pallas_call(kernel, out_shape=(jax.ShapeDtypeStruct((J * NW * 8, R), F...]
where the time goes in v5:
time: 161 us
  Pallas kernels  160 us (99%)
    pallas_call x1, Pallas kernels, body(): pl.pallas_call(kernel, out_shape=(jax.ShapeDtypeStruct((J * NW * 8, R), F...  158 us

profile of v5, /device:TPU:1, one launch (start us, length us, event | category | flops | bytes accessed | tf_op | source)
XLA Modules:
  0.0 160.9 jit_solution(3797907161117173144)
XLA Ops:
  0.6 158.5 %shard_map.75 = (f32[384,64]{1,0:T(8,128)}, f32[64,384]{1,0:T(8,128)}, f32[64,512]{1,0:T(8,128)}, f32[64,128]{1,0:T(8,128)}) custom-call(f32[11,24,4,8,128]{4,3,2,1,0:T(8,128)} %bitcast.7, f32[64,384]{1,0:T(8,128)} %bitcast.9, f32[64,512]{1,0:T(8,128)} %bitcast.8, f32[64,128]{1,0:T(8,128)} %bitcast.10), custom_call_target="tpu_custom_call" | custom-call | tf_op jit(solution)/shard_map/pallas_call | solution.py:454
  159.1 1.8 %shard_map.76 = (f32[11,4,4,64]{3,2,1,0:T(4,128)}, f32[64,384]{1,0:T(8,128)}, f32[64,512]{1,0:T(8,128)}, f32[64,128]{1,0:T(8,128)}) custom-call(f32[384,64]{1,0:T(8,128)} %get-tuple-element.12.core, f32[64,384]{1,0:T(8,128)} %get-tuple-element.13.fx, f32[64,512]{1,0:T(8,128)} %get-tuple-element.14.fy, f32[64,128]{1,0:T(8,128)} %get-tuple-element.15.fz), custom_call_target="tpu_custom_call" | custom-call | tf_op jit(solution)/shard_map/pallas_call | solution.py:439
